TPU v7x, 512 devices: a whole 4x4x16 slice. The times are simulated.
512 devices in a mesh: seq: 64 (over y, z), head: 8 (over x, core).
Axes of the slice: x: 4, y: 4, z: 16, core: 2. Of those that a mesh axis runs over, the one named last changes fastest.
Arguments:
- hidden_in: bfloat16 [16384, 4096], P('seq', 'head'), may hold values from -6 to 6
- proj_weight: bfloat16 [4096, 256], replicated, may hold values from -0.09375 to 0.09375
- head_input: bfloat16 [16384, 8192], P('seq', 'head'), may hold values from -6 to 6
- gate_input: bfloat16 [16384, 8192], P('seq', 'head'), may hold values from -11 to 11
- step_size: float32 [16384, 128], P('seq', 'head'), may hold values from 0 to 4, as said below
- decay_rate: float32 [128], P('head'), may hold values from 0 to 1, as said below
- norm_gain: float32 [8192], P('head'), may hold values from 0.1 to 1.9
Outputs:
- layer_out: bfloat16 [16384, 8192], P('seq', 'head')
Inputs may be any that keep to these rules, and one draw needn't show every extreme that they name: `decay_rate`: positive. `step_size`: positive.
All inputs are finite; a program needn't handle non-finite values.
Results may differ from a plain program's by a relative error of at most 0.013.
Values may be sent and summed in bfloat16 or wider, within the bound.
A program may use at most 128 MiB of HBM per device.

v0:
```python
import jax
import jax.numpy as jnp
from jax import lax
from jax.sharding import PartitionSpec as P

HEADS = 128
HEAD_DIM = 64
STATE = 128
GROUP = 256


def carried_in(value, axis, join, neutral):
    count, mine = (lax.axis_size(axis), lax.axis_index(axis))
    pieces = jax.tree.map(lambda part: lax.all_gather(part, axis), value)
    running = jax.tree.map(
        lambda part, zero: jnp.full_like(part, 0) + jnp.asarray(zero, part.dtype), value, neutral
    )

    def step(position, running):
        longer = join(running, jax.tree.map(lambda part: part[position], pieces))
        return jax.tree.map(lambda new, old: jnp.where(position < mine, new, old), longer, running)

    return lax.fori_loop(0, count - 1, step, running)


def combine_states(earlier, later):
    return (earlier[0] + later[0], jnp.exp(later[0])[:, None, None] * earlier[1] + later[1])


def shards(hidden_in, proj_weight, head_input, gate_input, step_size, decay_rate, norm_gain):
    tok_rows = hidden_in.shape[0]
    local_heads = step_size.shape[1]
    summed = jnp.dot(
        lax.all_gather(hidden_in, "head", axis=1, tiled=True),
        proj_weight,
        preferred_element_type=jnp.float32,
    )
    projected = summed.astype(jnp.bfloat16)
    count = tok_rows // GROUP
    b_rows = projected[:, :STATE].reshape(count, GROUP, STATE)
    c_rows = projected[:, STATE:].reshape(count, GROUP, STATE)
    log_decay = -step_size * decay_rate[None, :]
    cumulative = jnp.cumsum(log_decay.reshape(count, GROUP, local_heads), axis=1)
    scaled = (
        head_input.reshape(tok_rows, local_heads, HEAD_DIM).astype(jnp.float32)
        * step_size[:, :, None]
    ).astype(jnp.bfloat16)
    scaled = scaled.reshape(count, GROUP, local_heads, HEAD_DIM)
    positions = jnp.arange(GROUP, dtype=jnp.int32)
    causal = positions[:, None] >= positions[None, :]
    scores = jnp.einsum("ctn,csn->cts", c_rows, b_rows, preferred_element_type=jnp.float32)
    cum_heads = jnp.swapaxes(cumulative, 1, 2)
    gap = cum_heads[:, :, :, None] - cum_heads[:, :, None, :]
    weights = jnp.exp(jnp.where(causal[None, None], gap, -jnp.inf))
    mixing = (scores[:, None] * weights).astype(jnp.bfloat16)
    inner = jnp.einsum("chts,cshp->cthp", mixing, scaled, preferred_element_type=jnp.float32)
    ends = cumulative[:, -1, :]
    tail = jnp.exp(ends[:, None, :] - cumulative)
    weighted = (tail[:, :, :, None] * scaled.astype(jnp.float32)).astype(jnp.bfloat16)
    fresh = jnp.einsum("cshp,csn->chpn", weighted, b_rows, preferred_element_type=jnp.float32)
    block_state = jnp.zeros((local_heads, HEAD_DIM, STATE), jnp.float32)
    block_state = jnp.exp(ends[0])[:, None, None] * block_state + fresh[0]
    block_decay = jnp.sum(ends, axis=0)
    identity = (
        jnp.zeros((local_heads,), jnp.float32),
        jnp.zeros((local_heads, HEAD_DIM, STATE), jnp.float32),
    )
    decay_total, incoming = carried_in((block_decay, block_state), "seq", combine_states, identity)
    entering = [incoming]
    carried_low = jnp.stack(entering).astype(jnp.bfloat16)
    outer = jnp.einsum("ctn,chpn->cthp", c_rows, carried_low, preferred_element_type=jnp.float32)
    outer = outer * jnp.exp(cumulative)[:, :, :, None]
    mixed = (inner + outer).reshape(tok_rows, local_heads * HEAD_DIM)
    gated = mixed * jax.nn.silu(gate_input.astype(jnp.float32))
    squares = jnp.sum(gated * gated, axis=1)
    total_squares = lax.psum(squares, "head")
    mean_square = total_squares / (HEADS * HEAD_DIM)
    return (gated * lax.rsqrt(mean_square + 1e-05)[:, None] * norm_gain[None, :]).astype(
        jnp.bfloat16
    )


def solution(mesh):
    in_specs = (
        P("seq", "head"),
        P(),
        P("seq", "head"),
        P("seq", "head"),
        P("seq", "head"),
        P("head"),
        P("head"),
    )
    out_specs = P("seq", "head")
    return jax.shard_map(shards, mesh=mesh, in_specs=in_specs, out_specs=out_specs, check_vma=False)
```

profile of v0, /device:TPU:1, one launch (start us, length us, event | category | flops | bytes accessed | tf_op | source)
XLA Modules:
  0.0 524.2 jit_solution(10919568476322371059)
XLA Ops:
  9.5 1.2 copy.29
  11.6 36.5 %all-gather.5.cloned.1.call-done = bf16[256,4096]{1,0:T(8,128)(2,1)} async-done(((bf16[256,512]{1,0:T(8,128)(2,1)}), bf16[256,4096]{1,0:T(8,128)(2,1)}) %all-gather.5.cloned.1.call-update) | async-done | bytes 2097168 | tf_op jit(solution)/shard_map/all_gather | solution.py:34
  48.1 2.3 convolution_convert_fusion
  52.3 70.7 %all-gather = f32[64,1,16]{2,1,0:T(1,128)} all-gather(f32[1,1,16]{2,1,0:T(1,128)S(1)} %copy.34), channel_id=2, replica_groups=mesh['seq'=64,'head'=8] {'seq'}, dimensions={0}, use_global_device_ids=true | all-gather | bytes 4160 | tf_op jit(solution)/shard_map/all_gather | solution.py:14
  124.5 219.6 %all-gather.7.cloned.1.call-done = f32[1024,64,128]{2,1,0:T(8,128)} async-done(((f32[16,64,128]{2,1,0:T(8,128)}), f32[1024,64,128]{2,1,0:T(8,128)}) %all-gather.7.cloned.1.call-update) | async-done | bytes 33554448 | tf_op jit(solution)/shard_map/all_gather | solution.py:14
  344.1 150.7 %while.14 = (s32[]{:T(128)}, f32[16,64,128]{2,1,0:T(8,128)S(1)}, s32[]{:T(128)}, f32[64,16]{1,0:T(8,128)}, f32[64,16,64,128]{3,2,1,0:T(8,128)}, /*index=5*/s32[]{:T(128)}, s32[]{:T(128)}) while((s32[]{:T(128)}, f32[16,64,128]{2,1,0:T(8,128)S(1)}, s32[]{:T(128)}, f32[64,16]{1,0:T(8,128)}, f32[64,16,64,128]{3,2,1,0:T(8,128)}, ...), condition=%wide.region_3.4_spmd.clone, body=%wide.region_2.3_spmd.clone.sunk | while | flops 524292 | bytes 1573161 | solution.py:23
  344.1 1.2 exponential_bitcast_fusion.2
  346.5 1.2 exponential_bitcast_fusion.2
  348.9 1.2 exponential_bitcast_fusion.2
  351.3 1.2 exponential_bitcast_fusion.2
  353.7 1.2 exponential_bitcast_fusion.2
  356.1 1.2 exponential_bitcast_fusion.2
  358.5 1.2 exponential_bitcast_fusion.2
  360.9 1.2 exponential_bitcast_fusion.2
  363.2 1.2 exponential_bitcast_fusion.2
  365.6 1.2 exponential_bitcast_fusion.2
  368.0 1.2 exponential_bitcast_fusion.2
  370.4 1.2 exponential_bitcast_fusion.2
  372.8 1.2 exponential_bitcast_fusion.2
  375.2 1.2 exponential_bitcast_fusion.2
  377.6 1.2 exponential_bitcast_fusion.2
  380.0 1.2 exponential_bitcast_fusion.2
  382.4 1.2 exponential_bitcast_fusion.2
  384.8 1.2 exponential_bitcast_fusion.2
  387.2 1.2 exponential_bitcast_fusion.2
  389.6 1.2 exponential_bitcast_fusion.2
  392.0 1.2 exponential_bitcast_fusion.2
  394.4 1.2 exponential_bitcast_fusion.2
  401.5 1.2 exponential_bitcast_fusion.2
  403.9 1.2 exponential_bitcast_fusion.2
  406.3 1.2 exponential_bitcast_fusion.2
  408.7 1.2 exponential_bitcast_fusion.2
  411.1 1.2 exponential_bitcast_fusion.2
  413.5 1.2 exponential_bitcast_fusion.2
  415.9 1.2 exponential_bitcast_fusion.2
  418.3 1.2 exponential_bitcast_fusion.2
  420.6 1.2 exponential_bitcast_fusion.2
  423.0 1.2 exponential_bitcast_fusion.2
  425.4 1.2 exponential_bitcast_fusion.2
  427.8 1.2 exponential_bitcast_fusion.2
  430.2 1.2 exponential_bitcast_fusion.2
  432.6 1.2 exponential_bitcast_fusion.2
  435.0 1.2 exponential_bitcast_fusion.2
  437.4 1.2 exponential_bitcast_fusion.2
  458.8 1.2 exponential_bitcast_fusion.2
  461.2 1.2 exponential_bitcast_fusion.2
  463.6 1.2 exponential_bitcast_fusion.2
  466.0 1.2 exponential_bitcast_fusion.2
  468.4 1.2 exponential_bitcast_fusion.2
  470.8 1.2 exponential_bitcast_fusion.2
  473.2 1.2 exponential_bitcast_fusion.2
  475.6 1.2 exponential_bitcast_fusion.2
  478.0 1.2 exponential_bitcast_fusion.2
  480.4 1.2 exponential_bitcast_fusion.2
  482.8 1.2 exponential_bitcast_fusion.2
  485.2 1.2 exponential_bitcast_fusion.2
  487.6 1.2 exponential_bitcast_fusion.2
  490.0 1.2 exponential_bitcast_fusion.2
  492.4 1.2 exponential_bitcast_fusion.2
  495.8 3.1 fusion.9
  498.9 1.6 copy.37
  500.5 1.4 multiply_reduce_fusion
  501.9 13.2 %psum.7 = f32[256]{0:T(256)S(1)} all-reduce(f32[256]{0:T(256)S(1)} %multiply_reduce_fusion), channel_id=1, replica_groups=mesh['seq'=64,'head'=8] {'head'}, use_global_device_ids=true, to_apply=%region_5.6 | all-reduce | flops 256 | bytes 2048 | tf_op jit(solution)/shard_map/psum | solution.py:76
  515.1 2.2 multiply_convert_fusion.6
  (107 shorter events, 93.7 us)
Async XLA Ops:
  6.5 41.6 %copy-start = (bf16[4096,256]{1,0:T(8,128)(2,1)S(1)}, bf16[4096,256]{1,0:T(8,128)(2,1)}, u32[]{:S(2)}) copy-start(bf16[4096,256]{1,0:T(8,128)(2,1)} %param.10) | copy-start | bytes 6291460
  6.5 41.6 %all-gather.5.cloned.1.call-start = ((), (), s32[]{:S(2)}) async-start(), calls=%async_computation | async-start | bytes 2359296 | tf_op jit(solution)/shard_map/all_gather | solution.py:34
  7.3 336.8 %all-gather.7.cloned.1.call-start = ((), (), s32[]{:S(2)}) async-start(), calls=%async_computation.1 | async-start | bytes 34078720 | tf_op jit(solution)/shard_map/all_gather | solution.py:14
  344.1 151.7 %copy-start.1 = (f32[256,16]{0,1:T(8,128)S(1)}, f32[256,16]{0,1:T(8,128)}, u32[]{:S(2)}) copy-start(f32[256,16]{0,1:T(8,128)} %param.13) | copy-start | bytes 49156
  495.8 19.3 %copy-start.2 = (f32[1024]{0:T(1024)S(1)}, f32[1024]{0:T(1024)}, u32[]{:S(2)}) copy-start(f32[1024]{0:T(1024)} %param.15) | copy-start | bytes 12292
Sparse Core Ops, SparseCore 0:
  9.5 38.6 all-gather.4
  51.7 292.3 all-gather.6
where the time goes:
time: 528 us; the launch traced here: 524 us
  waiting for transfers between devices  257 us (49%)
  blocking collectives  83.9 us (16%)
  other arithmetic  81 us (15%)
  local copies, waits for them, and re-layouts  79.9 us (15%)
  between operations  13.5 us (3%)
  matrix products  7.67 us (1%)
    all_gather x1, waiting for transfers between devices, carried_in(): pieces = jax.tree.map(lambda part: lax.all_gather(part, axis), value)  220 us
    exp x63, local copies, waits for them, and re-layouts, combine_states(): jnp.exp(later[0])[:, None, None] * earlier[1] + later[1]  75.8 us
    select_n x63, other arithmetic, step(): jnp.where(position < mine, new, old)  73.7 us
    all_gather x1, blocking collectives, carried_in(): pieces = jax.tree.map(lambda part: lax.all_gather(part, axis), value)  70.7 us
    all_gather x1, waiting for transfers between devices, shards(): lax.all_gather(hidden_in, 'head', axis=1, tiled=True)  36.5 us
    psum x1, blocking collectives, shards(): total_squares = lax.psum(squares, 'head')  13.2 us
  transfers between devices with their start and end apart: 2, of which 2 were waited for; matrix products, arithmetic and copies ran while one was open for 1% of the time, Pallas kernels for 0%

commit v1 on v0

--- a/solution.py
+++ b/solution.py
@@ -7,6 +7,11 @@
 HEAD_DIM = 64
 STATE = 128
 GROUP = 256
+
+
+def exchange_gather(value, mesh_axis, d):
+    sent = jnp.stack([value] * lax.axis_size(mesh_axis))
+    return jnp.concatenate(lax.all_to_all(sent, mesh_axis, 0, 0), axis=d)
 
 
 def carried_in(value, axis, join, neutral):
@@ -31,9 +36,7 @@
     tok_rows = hidden_in.shape[0]
     local_heads = step_size.shape[1]
     summed = jnp.dot(
-        lax.all_gather(hidden_in, "head", axis=1, tiled=True),
-        proj_weight,
-        preferred_element_type=jnp.float32,
+        exchange_gather(hidden_in, "head", 1), proj_weight, preferred_element_type=jnp.float32
     )
     projected = summed.astype(jnp.bfloat16)
     count = tok_rows // GROUP

time: 528 us -> 524 us (level)
  waiting for transfers between devices: 257 us -> 243 us
  starting transfers between devices: 0.04 us -> 11.2 us
    all_gather x1 -> x0, waiting for transfers between devices: 36.5 us -> none  [shards(): lax.all_gather(hidden_in, 'head', axis=1, tiled=True)]
    all_to_all x0 -> x1, waiting for transfers between devices: none -> 24.5 us  [exchange_gather(): return jnp.concatenate(lax.all_to_all(sent, mesh_axis, 0, 0), axis=d)]
    all_to_all x0 -> x1, starting transfers between devices: none -> 11.2 us  [exchange_gather(): return jnp.concatenate(lax.all_to_all(sent, mesh_axis, 0, 0), axis=d)]
where the time goes in v1:
time: 524 us; the launch traced here: 520 us
  waiting for transfers between devices  243 us (46%)
  blocking collectives  82.2 us (16%)
  local copies, waits for them, and re-layouts  81.5 us (16%)
  other arithmetic  79.6 us (15%)
  between operations  13.5 us (3%)
  starting transfers between devices  11.2 us (2%)
  matrix products  7.73 us (1%)
    all_gather x1, waiting for transfers between devices, carried_in(): pieces = jax.tree.map(lambda part: lax.all_gather(part, axis), value)  219 us
    exp x63, local copies, waits for them, and re-layouts, combine_states(): jnp.exp(later[0])[:, None, None] * earlier[1] + later[1]  75.8 us
    select_n x63, other arithmetic, step(): jnp.where(position < mine, new, old)  73.7 us
    all_gather x1, blocking collectives, carried_in(): pieces = jax.tree.map(lambda part: lax.all_gather(part, axis), value)  69 us
    all_to_all x1, waiting for transfers between devices, exchange_gather(): return jnp.concatenate(lax.all_to_all(sent, mesh_axis, 0, 0), axis=d)  24.5 us
    psum x1, blocking collectives, shards(): total_squares = lax.psum(squares, 'head')  13.2 us
    all_to_all x1, starting transfers between devices, exchange_gather(): return jnp.concatenate(lax.all_to_all(sent, mesh_axis, 0, 0), axis=d)  11.2 us
  transfers between devices with their start and end apart: 2, of which 2 were waited for; matrix products, arithmetic and copies ran while one was open for 1% of the time, Pallas kernels for 0%

profile of v1, /device:TPU:1, one launch (start us, length us, event | category | flops | bytes accessed | tf_op | source)
XLA Modules:
  0.0 520.3 jit_solution(12702129873526778517)
XLA Ops:
  6.5 1.2 copy.32
  7.8 1.4 stack.2
  9.2 11.2 %all-to-all-start = ((bf16[8,256,512]{1,2,0:T(8,128)(2,1)}), bf16[8,256,512]{1,2,0:T(8,128)(2,1)}, u32[]{:S(2)}, u32[]{:S(2)}) async-start(bf16[8,256,512]{1,2,0:T(8,128)(2,1)} %stack.2), calls=%async_computation | async-start | bytes 4194304 | tf_op jit(solution)/shard_map/all_to_all | solution.py:14
  22.3 24.5 %all-to-all-done = bf16[8,256,512]{1,2,0:T(8,128)(2,1)} async-done(((bf16[8,256,512]{1,2,0:T(8,128)(2,1)}), bf16[8,256,512]{1,2,0:T(8,128)(2,1)}, u32[]{:S(2)}, u32[]{:S(2)}) %all-to-all-start) | async-done | bytes 2097184 | tf_op jit(solution)/shard_map/all_to_all | solution.py:14
  46.7 2.3 convolution_convert_fusion
  50.9 69.0 %all-gather = f32[64,1,16]{2,1,0:T(1,128)} all-gather(f32[1,1,16]{2,1,0:T(1,128)S(1)} %copy.37), channel_id=2, replica_groups=mesh['seq'=64,'head'=8] {'seq'}, dimensions={0}, use_global_device_ids=true | all-gather | bytes 4160 | tf_op jit(solution)/shard_map/all_gather | solution.py:19
  121.4 218.8 %all-gather.4.cloned.1.call-done = f32[1024,64,128]{2,1,0:T(8,128)} async-done(((f32[16,64,128]{2,1,0:T(8,128)}), f32[1024,64,128]{2,1,0:T(8,128)}) %all-gather.4.cloned.1.call-update) | async-done | bytes 33554448 | tf_op jit(solution)/shard_map/all_gather | solution.py:19
  340.2 150.7 %while.14 = (s32[]{:T(128)}, f32[16,64,128]{2,1,0:T(8,128)S(1)}, s32[]{:T(128)}, f32[64,16]{1,0:T(8,128)}, f32[64,16,64,128]{3,2,1,0:T(8,128)}, /*index=5*/s32[]{:T(128)}, s32[]{:T(128)}) while((s32[]{:T(128)}, f32[16,64,128]{2,1,0:T(8,128)S(1)}, s32[]{:T(128)}, f32[64,16]{1,0:T(8,128)}, f32[64,16,64,128]{3,2,1,0:T(8,128)}, ...), condition=%wide.region_3.4_spmd.clone, body=%wide.region_2.3_spmd.clone.sunk | while | flops 524292 | bytes 1573161 | solution.py:28
  340.2 1.2 exponential_bitcast_fusion.2
  342.6 1.2 exponential_bitcast_fusion.2
  345.0 1.2 exponential_bitcast_fusion.2
  347.4 1.2 exponential_bitcast_fusion.2
  349.8 1.2 exponential_bitcast_fusion.2
  352.2 1.2 exponential_bitcast_fusion.2
  354.6 1.2 exponential_bitcast_fusion.2
  357.0 1.2 exponential_bitcast_fusion.2
  359.4 1.2 exponential_bitcast_fusion.2
  361.8 1.2 exponential_bitcast_fusion.2
  364.2 1.2 exponential_bitcast_fusion.2
  366.6 1.2 exponential_bitcast_fusion.2
  369.0 1.2 exponential_bitcast_fusion.2
  371.4 1.2 exponential_bitcast_fusion.2
  373.8 1.2 exponential_bitcast_fusion.2
  376.2 1.2 exponential_bitcast_fusion.2
  378.6 1.2 exponential_bitcast_fusion.2
  380.9 1.2 exponential_bitcast_fusion.2
  383.3 1.2 exponential_bitcast_fusion.2
  385.7 1.2 exponential_bitcast_fusion.2
  397.7 1.2 exponential_bitcast_fusion.2
  400.0 1.2 exponential_bitcast_fusion.2
  402.4 1.2 exponential_bitcast_fusion.2
  404.8 1.2 exponential_bitcast_fusion.2
  407.2 1.2 exponential_bitcast_fusion.2
  409.6 1.2 exponential_bitcast_fusion.2
  412.0 1.2 exponential_bitcast_fusion.2
  414.4 1.2 exponential_bitcast_fusion.2
  416.8 1.2 exponential_bitcast_fusion.2
  419.2 1.2 exponential_bitcast_fusion.2
  421.6 1.2 exponential_bitcast_fusion.2
  423.9 1.2 exponential_bitcast_fusion.2
  426.3 1.2 exponential_bitcast_fusion.2
  428.7 1.2 exponential_bitcast_fusion.2
  431.1 1.2 exponential_bitcast_fusion.2
  433.5 1.2 exponential_bitcast_fusion.2
  455.0 1.2 exponential_bitcast_fusion.2
  457.4 1.2 exponential_bitcast_fusion.2
  459.8 1.2 exponential_bitcast_fusion.2
  462.2 1.2 exponential_bitcast_fusion.2
  464.6 1.2 exponential_bitcast_fusion.2
  466.9 1.2 exponential_bitcast_fusion.2
  469.3 1.2 exponential_bitcast_fusion.2
  471.7 1.2 exponential_bitcast_fusion.2
  474.1 1.2 exponential_bitcast_fusion.2
  476.5 1.2 exponential_bitcast_fusion.2
  478.9 1.2 exponential_bitcast_fusion.2
  481.3 1.2 exponential_bitcast_fusion.2
  483.7 1.2 exponential_bitcast_fusion.2
  486.1 1.2 exponential_bitcast_fusion.2
  488.5 1.2 exponential_bitcast_fusion.2
  491.9 3.1 fusion.9
  495.0 1.6 copy.40
  496.6 1.4 multiply_reduce_fusion
  498.1 13.2 %psum.7 = f32[256]{0:T(256)S(1)} all-reduce(f32[256]{0:T(256)S(1)} %multiply_reduce_fusion), channel_id=1, replica_groups=mesh['seq'=64,'head'=8] {'head'}, use_global_device_ids=true, to_apply=%region_5.6 | all-reduce | flops 256 | bytes 2048 | tf_op jit(solution)/shard_map/psum | solution.py:79
  511.2 2.2 multiply_convert_fusion.6
  (112 shorter events, 94.2 us)
Async XLA Ops:
  6.5 40.2 %copy-start = (bf16[4096,256]{1,0:T(8,128)(2,1)S(1)}, bf16[4096,256]{1,0:T(8,128)(2,1)}, u32[]{:S(2)}) copy-start(bf16[4096,256]{1,0:T(8,128)(2,1)} %param.10) | copy-start | bytes 6291460
  9.2 11.2 %copy-start.2 = (f32[256,16]{0,1:T(8,128)S(1)}, f32[256,16]{0,1:T(8,128)}, u32[]{:S(2)}) copy-start(f32[256,16]{0,1:T(8,128)} %param.13) | copy-start | bytes 49156
  9.2 11.2 %copy-start.4 = (f32[16]{0:T(128)S(1)}, f32[16]{0:T(128)}, u32[]{:S(2)}) copy-start(f32[16]{0:T(128)} %param.14) | copy-start | bytes 196
  9.2 12.7 %copy-start.1 = (bf16[256,1024]{1,0:T(8,128)(2,1)S(1)}, bf16[256,1024]{1,0:T(8,128)(2,1)}, u32[]{:S(2)}) copy-start(bf16[256,1024]{1,0:T(8,128)(2,1)} %param.11) | copy-start | bytes 1572868
  9.2 37.5 %all-to-all-start = ((bf16[8,256,512]{1,2,0:T(8,128)(2,1)}), bf16[8,256,512]{1,2,0:T(8,128)(2,1)}, u32[]{:S(2)}, u32[]{:S(2)}) async-start(bf16[8,256,512]{1,2,0:T(8,128)(2,1)} %stack.2), calls=%async_computation | async-start | bytes 4194304 | tf_op jit(solution)/shard_map/all_to_all | solution.py:14
  20.4 319.8 %all-gather.4.cloned.1.call-start = ((), (), s32[]{:S(2)}) async-start(), calls=%async_computation.1 | async-start | bytes 34078720 | tf_op jit(solution)/shard_map/all_gather | solution.py:19
  495.0 16.2 %copy-start.3 = (f32[1024]{0:T(1024)S(1)}, f32[1024]{0:T(1024)}, u32[]{:S(2)}) copy-start(f32[1024]{0:T(1024)} %param.15) | copy-start | bytes 12292
Sparse Core Ops, SparseCore 0:
  50.3 289.8 all-gather.3
